TPU v7x, 32 devices: a whole 2x2x4 slice. The times are simulated.
32 devices in a mesh: blk: 8 (over y, x, core), req: 4 (over z).
Axes of the slice: x: 2, y: 2, z: 4, core: 2. Of those that a mesh axis runs over, the one named last changes fastest.
Arguments:
- verified_queries: bfloat16 [4, 16, 5, 1024], P('req', 'blk'), may hold values from -96 to 96
- new_keys: bfloat16 [4, 16, 5, 256], P('req', 'blk'), may hold values from -6 to 6
- verified_value_rows: bfloat16 [4, 16, 5, 256], P('req', 'blk'), may hold values from -6 to 6
- prior_round_keys: bfloat16 [4, 16, 5, 256], P('req', 'blk'), may hold values from -6 to 6
- prior_round_values: bfloat16 [4, 16, 5, 256], P('req', 'blk'), may hold values from -6 to 6
- accepted: int32 [4, 16], P('req', 'blk'), may hold values from 0 to 5
- group_id: int32 [4, 16], P('req'), may hold values from 0 to 15
- cache_len: int32 [4, 16], P('req'), may hold values from 0 to 8192, as said below
- slot_owner: int32 [4, 64], P('req'), may hold values from 0 to 15, as said below
- piece_cache_keys: bfloat16 [4, 64, 256, 256], P('req', 'blk'), may hold values from -6 to 6
- piece_cache_values: bfloat16 [4, 64, 256, 256], P('req', 'blk'), may hold values from -6 to 6
- shared_prompt_keys: bfloat16 [16, 256, 256], P('req', 'blk'), may hold values from -6 to 6
- shared_prompt_values: bfloat16 [16, 256, 256], P('req', 'blk'), may hold values from -6 to 6
- prompt_mask: int32 [16, 8], P('req', 'blk'), may hold values 0 or 1
Outputs:
- attended: bfloat16 [4, 16, 5, 1024], P('req', 'blk')
Inputs may be any that keep to these rules, and one draw needn't show every extreme that they name: `slot_owner`: A request's cache is the concatenation, in piece order, of the pieces that name it. In every batch one request owns exactly 32 pieces and no request owns more. `cache_len`: A request's length is at most 256 times the number of pieces it owns and more than 256 times one fewer; in every batch one request holds exactly 8192 rows.
All inputs are finite; a program needn't handle non-finite values. No bound on the sum of `prompt_mask` on one device may be relied on, other than what follows from the above.
Results may differ from a plain program's by a relative error of at most 0.003.
Values may be sent and summed in bfloat16 or wider, within the bound.
No kernel may reach another device: no remote copies, remote signals or barrier semaphores. Data moves between devices by JAX's collectives and lax.ppermute only.
A program may use at most 64 MiB of HBM per device.

v0:
```python
import jax
import jax.numpy as jnp
from jax import lax
from jax.sharding import PartitionSpec as P

QUERY_HEADS = 16
KEY_HEADS = 4
HEAD_SIZE = 64
VERIFIED_COUNT = 5
LOWEST = -1e30


def block_weights(scores, live_rows):
    masked = jnp.where(live_rows, scores, LOWEST)
    ceiling = jnp.max(masked, axis=-1)
    weights = jnp.where(live_rows, jnp.exp(masked - ceiling[..., None]), 0.0).astype(jnp.bfloat16)
    return (ceiling, weights, jnp.sum(weights.astype(jnp.float32), axis=-1))


def per_device(
    verified_queries,
    new_keys,
    verified_value_rows,
    prior_round_keys,
    prior_round_values,
    accepted,
    group_id,
    cache_len,
    slot_owner,
    piece_cache_keys,
    piece_cache_values,
    shared_prompt_keys,
    shared_prompt_values,
    prompt_mask,
):
    position_here = lax.axis_index("blk")
    request_rows = verified_queries.shape[1]
    rows_of_batch = group_id.shape[1]
    local_pieces = piece_cache_keys.shape[1]
    rows_of_piece = piece_cache_keys.shape[2]
    heads_per_key = QUERY_HEADS // KEY_HEADS
    score_scale = HEAD_SIZE ** (-0.5)
    row_lanes = QUERY_HEADS * VERIFIED_COUNT
    highest = lax.Precision.HIGHEST
    every_query = lax.all_gather(verified_queries, "blk", axis=1, tiled=True)[0].reshape(
        rows_of_batch, VERIFIED_COUNT, KEY_HEADS, heads_per_key, HEAD_SIZE
    )
    owners = slot_owner[0]
    requests_all = jnp.arange(rows_of_batch, dtype=jnp.int32)
    owner_table = (owners[:, None] == requests_all[None, :]).astype(jnp.int32)
    before = jnp.cumsum(owner_table, axis=0) - owner_table
    ranking = jnp.sum(before * owner_table, axis=1)
    filling = jnp.clip(cache_len[0][owners] - ranking * rows_of_piece, 0, rows_of_piece)
    my_owner = lax.dynamic_slice_in_dim(owners, position_here * local_pieces, local_pieces)
    my_fill = lax.dynamic_slice_in_dim(filling, position_here * local_pieces, local_pieces)
    slot_query = every_query[my_owner]
    keys_of_slot = piece_cache_keys[0].reshape(local_pieces, rows_of_piece, KEY_HEADS, HEAD_SIZE)
    values_of_slot = piece_cache_values[0].reshape(
        local_pieces, rows_of_piece, KEY_HEADS, HEAD_SIZE
    )
    scores = (
        jnp.einsum(
            "snkgd,sjkd->skgnj", slot_query, keys_of_slot, preferred_element_type=jnp.float32
        )
        * score_scale
    )
    live_piece = jnp.arange(rows_of_piece, dtype=jnp.int32)[None, :] < my_fill[:, None]
    live_rows = jnp.broadcast_to(live_piece[:, None, None, None, :], scores.shape)
    slot_top, slot_weights, slot_mass = block_weights(scores, live_rows)
    slot_part = jnp.einsum(
        "skgnj,sjkd->skgnd", slot_weights, values_of_slot, preferred_element_type=jnp.float32
    )
    collected_keys, collected_values, gathered_live = (
        lax.all_gather(shared_prompt_keys, "req", axis=0, tiled=True),
        lax.all_gather(shared_prompt_values, "req", axis=0, tiled=True),
        lax.all_gather(prompt_mask[:, 0].astype(jnp.bfloat16), "req", axis=0, tiled=True),
    )
    prompt_groups = group_id[0]
    keys_of_block = collected_keys[prompt_groups].reshape(rows_of_batch, -1, KEY_HEADS, HEAD_SIZE)
    values_of_block = collected_values[prompt_groups].reshape(
        rows_of_batch, -1, KEY_HEADS, HEAD_SIZE
    )
    block_live = gathered_live[prompt_groups] > 0.5
    scores = (
        jnp.einsum(
            "rnkgd,rjkd->rkgnj", every_query, keys_of_block, preferred_element_type=jnp.float32
        )
        * score_scale
    )
    live_rows = jnp.broadcast_to(block_live[:, None, None, None, None], scores.shape)
    prompt_top, prompt_weights, prompt_mass = block_weights(scores, live_rows)
    prompt_part = jnp.einsum(
        "rkgnj,rjkd->rkgnd", prompt_weights, values_of_block, preferred_element_type=jnp.float32
    )
    choose = my_owner[:, None] == requests_all[None, :]
    picked = choose.astype(jnp.float32)
    slot_flat = slot_top.reshape(local_pieces, row_lanes)
    prompt_flat = prompt_top.reshape(rows_of_batch, row_lanes)
    slot_best = jnp.max(jnp.where(choose[:, :, None], slot_flat[:, None, :], LOWEST), axis=0)
    device_top = jnp.maximum(slot_best, prompt_flat)
    overall_top = lax.pmax(device_top, "blk")
    slot_lift = jnp.exp(slot_flat - overall_top[my_owner])
    slot_terms = (
        slot_lift[..., None] * slot_part.reshape(local_pieces, row_lanes, HEAD_SIZE)
    ).reshape(local_pieces, row_lanes * HEAD_SIZE)
    prompt_lift = jnp.exp(prompt_flat - overall_top)
    numerator = jnp.dot(picked.T, slot_terms, precision=highest) + (
        prompt_lift[..., None] * prompt_part.reshape(rows_of_batch, row_lanes, HEAD_SIZE)
    ).reshape(rows_of_batch, row_lanes * HEAD_SIZE)
    denominator = jnp.dot(
        picked.T, slot_lift * slot_mass.reshape(local_pieces, row_lanes), precision=highest
    ) + prompt_lift * prompt_mass.reshape(rows_of_batch, row_lanes)
    numerator, denominator = (numerator, denominator)
    got_numerator, got_denominator = (
        lax.psum_scatter(numerator, "blk", scatter_dimension=0, tiled=True),
        lax.psum_scatter(denominator, "blk", scatter_dimension=0, tiled=True),
    )
    got_top = lax.dynamic_slice_in_dim(overall_top, position_here * request_rows, request_rows)
    request_query = verified_queries[0].reshape(
        request_rows, VERIFIED_COUNT, KEY_HEADS, heads_per_key, HEAD_SIZE
    )
    request_keys = jnp.concatenate([prior_round_keys[0], new_keys[0]], axis=1).reshape(
        request_rows, 2 * VERIFIED_COUNT, KEY_HEADS, HEAD_SIZE
    )
    request_values = jnp.concatenate(
        [prior_round_values[0], verified_value_rows[0]], axis=1
    ).reshape(request_rows, 2 * VERIFIED_COUNT, KEY_HEADS, HEAD_SIZE)
    scores = (
        jnp.einsum(
            "rnkgd,rjkd->rkgnj", request_query, request_keys, preferred_element_type=jnp.float32
        )
        * score_scale
    )
    column = jnp.arange(2 * VERIFIED_COUNT, dtype=jnp.int32)
    position = jnp.arange(VERIFIED_COUNT, dtype=jnp.int32)
    live_prev = (column[None, :] < VERIFIED_COUNT) & (column[None, :] < accepted[0][:, None])
    live_new = (column[None, :] >= VERIFIED_COUNT) & (
        column[None, :] - VERIFIED_COUNT <= position[:, None]
    )
    live_rows = live_prev[:, None, None, None, :] | live_new[None, None, None, :, :]
    own_top, own_weights, own_mass = block_weights(scores, live_rows)
    own_part = jnp.einsum(
        "rkgnj,rjkd->rkgnd", own_weights, request_values, preferred_element_type=jnp.float32
    )
    own_flat = own_top.reshape(request_rows, row_lanes)
    best_top = jnp.maximum(got_top, own_flat)
    far_lift = jnp.exp(got_top - best_top)
    near_lift = jnp.exp(own_flat - best_top)
    overall_mass = far_lift * got_denominator + near_lift * own_mass.reshape(
        request_rows, row_lanes
    )
    overall_part = far_lift[..., None] * got_numerator.reshape(
        request_rows, row_lanes, HEAD_SIZE
    ) + near_lift[..., None] * own_part.reshape(request_rows, row_lanes, HEAD_SIZE)
    attention_output = (overall_part / overall_mass[..., None]).reshape(
        request_rows, KEY_HEADS, heads_per_key, VERIFIED_COUNT, HEAD_SIZE
    )
    return (
        attention_output.transpose(0, 3, 1, 2, 4)
        .reshape(1, request_rows, VERIFIED_COUNT, QUERY_HEADS * HEAD_SIZE)
        .astype(jnp.bfloat16)
    )


def solution(mesh):
    placed = (
        P("req", "blk", None, None),
        P("req", "blk", None, None),
        P("req", "blk", None, None),
        P("req", "blk", None, None),
        P("req", "blk", None, None),
        P("req", "blk"),
        P("req", None),
        P("req", None),
        P("req", None),
        P("req", "blk", None, None),
        P("req", "blk", None, None),
        P("req", "blk", None),
        P("req", "blk", None),
        P("req", "blk"),
    )
    return jax.shard_map(
        per_device,
        mesh=mesh,
        in_specs=placed,
        out_specs=P("req", "blk", None, None),
        check_vma=False,
    )
```

profile of v0, /device:TPU:0, one launch (start us, length us, event | category | flops | bytes accessed | tf_op | source)
XLA Modules:
  0.0 155.7 jit_solution(5203253228424417421)
XLA Ops:
  6.5 0.7 copy-done.18
  7.3 0.6 copy-done.24
  7.9 0.7 copy-done.25
  8.5 0.6 copy-done.28
  9.2 0.6 dynamic-slice.1
  10.7 13.4 %all-reduce = bf16[16]{0:T(256)(128)(2,1)S(1)} all-reduce(bf16[16]{0:T(256)(128)(2,1)S(1)} %dynamic-update-slice), channel_id=2, replica_groups=mesh['blk'=8,'req'=4] {'req'}, use_global_device_ids=true, to_apply=%add | all-reduce | flops 16 | bytes 64 | tf_op jit(solution)/shard_map/all_gather | solution.py:76
  24.3 0.7 gather_fusion.2
  25.4 0.8 gather_fusion
  26.3 9.3 %all_gather.12 = bf16[1,16,5,1024]{3,2,0,1:T(8,128)(2,1)S(1)} all-gather(bf16[1,2,5,1024]{3,2,0,1:T(8,128)(2,1)S(1)} %copy.55), channel_id=1, replica_groups=mesh['blk'=8,'req'=4] {'blk'}, dimensions={1}, use_global_device_ids=true | all-gather | bytes 184320 | tf_op jit(solution)/shard_map/all_gather | solution.py:45
  36.0 0.6 copy-done.8
  36.6 14.4 %all_gather.14 = bf16[16,32,256]{2,1,0:T(8,128)(2,1)S(1)} all-gather(bf16[4,32,256]{2,1,0:T(8,128)(2,1)S(1)} %copy-done.8), channel_id=1, replica_groups=mesh['blk'=8,'req'=4] {'req'}, dimensions={0}, use_global_device_ids=true | all-gather | bytes 327680 | tf_op jit(solution)/shard_map/all_gather | solution.py:74
  51.0 0.6 gather_fusion.3
  51.8 0.7 gather_fusion.1
  52.5 1.5 fusion.40
  54.2 0.5 copy.57
  54.7 0.5 fusion.41
  55.5 12.2 %pmax.7 = f32[16,80]{1,0:T(8,128)S(1)} all-reduce(f32[16,80]{1,0:T(8,128)S(1)} %max.18), channel_id=1, replica_groups=mesh['blk'=8,'req'=4] {'blk'}, use_global_device_ids=true, to_apply=%region_5.6 | all-reduce | flops 1280 | bytes 10240 | tf_op jit(solution)/shard_map/pmax | solution.py:101
  67.7 0.6 subtract_exponential_fusion
  68.3 1.1 gather_fusion.4
  69.5 14.4 %all_gather.15 = bf16[16,32,256]{2,1,0:T(8,128)(2,1)S(1)} all-gather(bf16[4,32,256]{2,1,0:T(8,128)(2,1)S(1)} %copy-done.9), channel_id=1, replica_groups=mesh['blk'=8,'req'=4] {'req'}, dimensions={0}, use_global_device_ids=true | all-gather | bytes 327680 | tf_op jit(solution)/shard_map/all_gather | solution.py:75
  83.9 0.6 gather_fusion.5
  84.4 1.1 reshape.310
  85.5 0.6 copy-done.22
  86.1 1.7 %fusion.10 = f32[16,4,4,5,64]{4,3,2,1,0:T(8,128)S(1)} fusion(bf16[16,32,4,64,1]{3,2,1,0,4:T(4,128)(2,1)} %bitcast.77, f32[16,4,4,5,32]{4,3,2,1,0:T(8,128)S(1)} %copy-done.1, f32[16,4,4,5]{3,2,1,0:T(4,128)} %copy-done.4, pred[16]{0:T(512)(128)(4,1)S(1)} %copy-done.22), kind=kOutput, calls=%fused_computation.26 | convolution fusion | flops 5365760 | bytes 758800 | tf_op jit(solution)/shard_map/rkgnj,rjkd->rkgnd/dot_general | solution.py:92
  87.8 0.3 reshape.311
  88.1 0.4 copy-done.13
  88.8 0.6 copy-done.10
  89.8 1.5 copy.66
  91.3 0.7 copy-done.12
  92.0 0.5 fusion.17
  92.5 0.8 reshape.309
  93.3 2.1 %convolution_add_fusion = f32[16,5120]{1,0:T(8,128)} fusion(f32[16,5120]{1,0:T(8,128)S(1)} %mul.110, f32[16,5120]{1,0:T(8,128)S(1)} %reshape.311, f32[8,5120]{1,0:T(8,128)S(1)} %mul.107, f32[8,5120]{1,0:T(8,128)} %reshape.309, s32[8]{0:T(128)S(1)} %copy-done.20), kind=kOutput, calls=%fused_computation.6 | convolution fusion | flops 8069248 | bytes 1310752 | tf_op jit(solution)/shard_map/dot_general | solution.py:107
  95.4 0.7 copy-done.7
  96.3 0.4 copy-done.23
  96.7 0.8 convert_reduce_fusion
  97.5 0.5 convert_reduce_fusion.1
  98.0 0.7 copy-done.14
  98.8 0.7 copy-done.15
  99.5 0.7 copy-done.16
  100.3 0.7 copy-done.17
  101.1 0.6 copy-done.26
  102.8 0.3 convolution_add_fusion.1
  103.1 12.1 %all-reduce.2 = f32[16,80]{1,0:T(8,128)S(1)} all-reduce(f32[16,80]{1,0:T(8,128)S(1)} %convolution_add_fusion.1), channel_id=4, replica_groups=mesh['blk'=8,'req'=4] {'blk'}, use_global_device_ids=true, to_apply=%region_10.11.clone | all-reduce | flops 1280 | bytes 10240
  115.2 0.6 copy-done.27
  115.8 0.6 dynamic-slice.2
  117.4 29.5 %all-reduce.5.cloned.1.call-done = f32[16,5120]{1,0:T(8,128)} async-done(((f32[16,5120]{1,0:T(8,128)}), f32[16,5120]{1,0:T(8,128)}) %all-reduce.5.cloned.1.call-update) | async-done | bytes 327696
  146.8 0.9 constant_dynamic-slice_fusion
  148.1 0.7 convert_element_type.56
  (102 shorter events, 5.1 us)
Async XLA Ops:
  6.5 18.8 %copy-start = (s32[1,16]{1,0:T(1,128)S(1)}, s32[1,16]{1,0:T(1,128)}, u32[]{:S(2)}) copy-start(s32[1,16]{1,0:T(1,128)} %param.21) | copy-start | bytes 196
  6.5 140.3 %all-reduce.5.cloned.1.call-start = ((), (), s32[]{:S(2)}) async-start(), calls=%async_computation | async-start | bytes 655360
  6.5 0.7 copy-start.18
  7.2 0.7 copy-start.24
  7.9 16.3 %copy-start.19 = (s32[8]{0:T(128)}, s32[8]{0:T(128)S(1)}, u32[]{:S(2)}) copy-start(s32[8]{0:T(128)S(1)} %fusion.33) | copy-start | bytes 100
  7.9 0.7 copy-start.25
  8.5 0.7 copy-start.28
  24.3 0.7 copy-start.6
  24.9 27.6 %copy-start.21 = (pred[16]{0:T(512)(128)(4,1)}, pred[16]{0:T(512)(128)(4,1)S(1)}, u32[]{:S(2)}) copy-start(pred[16]{0:T(512)(128)(4,1)S(1)} %broadcast_compare_fusion) | copy-start | bytes 52
  26.3 28.4 %copy-start.11 = (pred[8,256]{1,0:T(8,128)(4,1)}, pred[8,256]{1,0:T(8,128)(4,1)S(1)}, u32[]{:S(2)}) copy-start(pred[8,256]{1,0:T(8,128)(4,1)S(1)} %iota_compare_fusion.1) | copy-start | bytes 6148
  35.7 0.8 copy-start.8
  52.5 1.6 %copy-start.3 = (bf16[1,8,256,256]{3,2,1,0:T(8,128)(2,1)S(1)}, bf16[1,8,256,256]{3,2,1,0:T(8,128)(2,1)}, u32[]{:S(2)}) copy-start(bf16[1,8,256,256]{3,2,1,0:T(8,128)(2,1)} %param.23) | copy-start | bytes 3145732
  54.0 0.7 copy-start.4
  54.7 14.8 %copy-start.9 = (bf16[4,32,256]{2,1,0:T(8,128)(2,1)S(1)}, bf16[4,32,256]{2,1,0:T(8,128)(2,1)}, u32[]{:S(2)}) copy-start(bf16[4,32,256]{2,1,0:T(8,128)(2,1)} %param.26) | copy-start | bytes 196612
  55.2 30.3 %copy-start.1 = (f32[16,4,4,5,32]{4,3,2,1,0:T(8,128)S(1)}, f32[16,4,4,5,32]{4,3,2,1,0:T(8,128)}, u32[]{:S(2)}) copy-start(f32[16,4,4,5,32]{4,3,2,1,0:T(8,128)} %get-tuple-element.9) | copy-start | bytes 491524
  85.5 0.6 copy-start.22
  87.8 0.7 copy-start.13
  88.7 0.7 copy-start.10
  91.3 0.7 copy-start.12
  92.0 1.3 copy-start.20
  92.5 3.7 %copy-start.2 = (f32[16,4,4,5,32]{4,3,2,1,0:T(8,128)S(1)}, f32[16,4,4,5,32]{4,3,2,1,0:T(8,128)}, u32[]{:S(2)}) copy-start(f32[16,4,4,5,32]{4,3,2,1,0:T(8,128)} %get-tuple-element.9) | copy-start | bytes 491524
  95.3 0.7 copy-start.7
  95.3 0.9 copy-start.5
  96.1 0.6 copy-start.23
  98.0 0.7 copy-start.14
  98.7 0.7 copy-start.15
  99.5 0.7 copy-start.16
  100.3 0.7 copy-start.17
  101.1 0.7 copy-start.26
  115.1 0.7 copy-start.27
Sparse Core Ops, SparseCore 0:
  95.5 51.2 all-reduce.4
where the time goes:
time: 156 us
  blocking collectives  75.9 us (49%)
  waiting for transfers between devices  29.5 us (19%)
  local copies, waits for them, and re-layouts  25.3 us (16%)
  between operations  15.1 us (10%)
  matrix products  7 us (4%)
  other arithmetic  2.93 us (2%)
    unnamed x2, waiting for transfers between devices  29.5 us
    unnamed x66, local copies, waits for them, and re-layouts  15 us
    all_gather x1, blocking collectives, per_device(): lax.all_gather(shared_prompt_keys, 'req', axis=0, tiled=True)  14.4 us
    all_gather x1, blocking collectives, per_device(): lax.all_gather(shared_prompt_values, 'req', axis=0, tiled=True)  14.4 us
    all_gather x1, blocking collectives, per_device(): lax.all_gather(prompt_mask[:, 0].astype(jnp.bfloat16), 'req', axis=0, til...  13.4 us
    pmax x1, blocking collectives, per_device(): overall_top = lax.pmax(device_top, 'blk')  12.2 us
    unnamed x1, blocking collectives  12.1 us
    all_gather x1, blocking collectives, per_device(): lax.all_gather(verified_queries, 'blk', axis=1, tiled=True)[0]  9.31 us
  transfers between devices with their start and end apart: 1, of which 1 were waited for; matrix products, arithmetic and copies ran while one was open for 3% of the time, Pallas kernels for 0%

commit v1 on v0

--- a/solution.py
+++ b/solution.py
@@ -8,6 +8,28 @@
 HEAD_SIZE = 64
 VERIFIED_COUNT = 5
 LOWEST = -1e30
+
+
+def laid_out(blocks, dim):
+    blocks = jnp.moveaxis(blocks, 0, dim)
+    shape = blocks.shape
+    return blocks.reshape(*shape[:dim], shape[dim] * shape[dim + 1], *shape[dim + 2 :])
+
+
+def grow_blocks(x, axis):
+    length = lax.axis_size(axis)
+    pieces = x[None]
+    for level in range(length.bit_length() - 1):
+        stride = 1 << level
+        received = lax.ppermute(pieces, axis, [(i, i ^ stride) for i in range(length)])
+        both = jnp.stack([pieces, received])
+        upper = lax.axis_index(axis) >> level & 1
+        pieces = jnp.where(upper == 0, both, both[::-1]).reshape(-1, *x.shape)
+    return pieces
+
+
+def doubled_up(array, axis, dim):
+    return laid_out(grow_blocks(array, axis), dim)
 
 
 def block_weights(scores, live_rows):
@@ -42,7 +64,7 @@
     score_scale = HEAD_SIZE ** (-0.5)
     row_lanes = QUERY_HEADS * VERIFIED_COUNT
     highest = lax.Precision.HIGHEST
-    every_query = lax.all_gather(verified_queries, "blk", axis=1, tiled=True)[0].reshape(
+    every_query = doubled_up(verified_queries, "blk", 1)[0].reshape(
         rows_of_batch, VERIFIED_COUNT, KEY_HEADS, heads_per_key, HEAD_SIZE
     )
     owners = slot_owner[0]

time: 156 us -> 179 us (1.15)
  waiting for transfers between devices: 29.5 us -> 52.8 us
  blocking collectives: 75.9 us -> 65.9 us
  starting transfers between devices: 0.01 us -> 3.6 us
  local copies, waits for them, and re-layouts: 25.3 us -> 28.7 us
  other arithmetic: 2.93 us -> 4.86 us
    unnamed x2, waiting for transfers between devices: 29.5 us -> 49.9 us
    all_gather x1 -> x0, blocking collectives: 9.31 us -> none  [per_device(): lax.all_gather(verified_queries, 'blk', axis=1, tiled=True)[0]]
    ppermute x0 -> x3, starting transfers between devices: none -> 3.6 us  [grow_blocks(): lax.ppermute(pieces, axis, [(i, i ^ stride) for i in range(length)])]
    ppermute x0 -> x3, waiting for transfers between devices: none -> 2.92 us  [grow_blocks(): lax.ppermute(pieces, axis, [(i, i ^ stride) for i in range(length)])]
    unnamed x66 -> x67, local copies, waits for them, and re-layouts: 15 us -> 15.8 us
  transfers between devices with their start and end apart: 1 -> 4, of which waited for: 1 -> 2; matrix products, arithmetic and copies ran while one was open for 3% -> 7% of each run, Pallas kernels for 0% -> 0%
where the time goes in v1:
time: 179 us; the launch traced here: 178 us
  blocking collectives  65.9 us (37%)
  waiting for transfers between devices  52.8 us (29%)
  local copies, waits for them, and re-layouts  28.7 us (16%)
  between operations  15.1 us (8%)
  matrix products  6.95 us (4%)
  other arithmetic  4.86 us (3%)
  starting transfers between devices  3.6 us (2%)
    unnamed x2, waiting for transfers between devices  49.9 us
    unnamed x67, local copies, waits for them, and re-layouts  15.8 us
    all_gather x1, blocking collectives, per_device(): lax.all_gather(shared_prompt_values, 'req', axis=0, tiled=True)  14.3 us
    all_gather x1, blocking collectives, per_device(): lax.all_gather(shared_prompt_keys, 'req', axis=0, tiled=True)  13.8 us
    all_gather x1, blocking collectives, per_device(): lax.all_gather(prompt_mask[:, 0].astype(jnp.bfloat16), 'req', axis=0, til...  13 us
    unnamed x1, blocking collectives  12.6 us
    pmax x1, blocking collectives, per_device(): overall_top = lax.pmax(device_top, 'blk')  12.2 us
    ppermute x3, starting transfers between devices, grow_blocks(): lax.ppermute(pieces, axis, [(i, i ^ stride) for i in range(length)])  3.6 us
  transfers between devices with their start and end apart: 4, of which 2 were waited for; matrix products, arithmetic and copies ran while one was open for 7% of the time, Pallas kernels for 0%

profile of v1, /device:TPU:0, one launch (start us, length us, event | category | flops | bytes accessed | tf_op | source)
XLA Modules:
  0.0 177.9 jit_solution(8978116276390751210)
XLA Ops:
  7.0 0.7 copy-done.20
  7.8 0.6 copy-done.25
  8.5 0.6 copy-done.26
  9.1 0.6 copy-done.29
  9.8 0.6 dynamic-slice.1
  11.4 13.0 %all-reduce = bf16[16]{0:T(256)(128)(2,1)S(1)} all-reduce(bf16[16]{0:T(256)(128)(2,1)S(1)} %dynamic-update-slice), channel_id=2, replica_groups=mesh['blk'=8,'req'=4] {'req'}, use_global_device_ids=true, to_apply=%add | all-reduce | flops 16 | bytes 64 | tf_op jit(solution)/shard_map/all_gather | solution.py:98
  24.4 0.7 gather_fusion.2
  25.2 0.7 copy-done.14
  25.9 0.7 copy-done.15
  27.1 0.8 gather_fusion
  28.0 0.7 copy-done.27
  29.9 0.6 copy-done.10
  30.5 13.8 %all_gather.10 = bf16[16,32,256]{2,1,0:T(8,128)(2,1)S(1)} all-gather(bf16[4,32,256]{2,1,0:T(8,128)(2,1)S(1)} %copy-done.10), channel_id=1, replica_groups=mesh['blk'=8,'req'=4] {'req'}, dimensions={0}, use_global_device_ids=true | all-gather | bytes 327680 | tf_op jit(solution)/shard_map/all_gather | solution.py:96
  44.4 1.6 collective-permute-start.1
  46.0 14.3 %all_gather.11 = bf16[16,32,256]{2,1,0:T(8,128)(2,1)S(1)} all-gather(bf16[4,32,256]{2,1,0:T(8,128)(2,1)S(1)} %copy-done.11), channel_id=1, replica_groups=mesh['blk'=8,'req'=4] {'req'}, dimensions={0}, use_global_device_ids=true | all-gather | bytes 327680 | tf_op jit(solution)/shard_map/all_gather | solution.py:97
  60.3 0.7 reshape.316
  61.0 0.7 copy-done.16
  61.8 0.7 copy-done.17
  62.6 0.7 reshape.323
  63.2 0.6 gather_fusion.3
  63.8 1.0 reshape.314
  64.9 0.6 gather_fusion.5
  65.4 1.0 reshape.318
  66.5 0.5 copy.59
  67.0 1.5 copy.68
  68.5 0.6 copy-done.28
  69.2 0.6 dynamic-slice.2
  70.5 1.6 collective-permute-start.2
  72.1 2.9 %collective-permute-done.2 = bf16[4,1,2,5,1024]{4,2,0,3,1:T(2,128)(2,1)S(1)} collective-permute-done((bf16[4,1,2,5,1024]{4,2,0,3,1:T(2,128)(2,1)S(1)}, bf16[4,1,2,5,1024]{4,2,0,3,1:T(2,128)(2,1)S(1)}, u32[]{:S(2)}, u32[]{:S(2)}) %collective-permute-start.2) | collective-permute-done | bytes 81952 | tf_op jit(solution)/shard_map/ppermute | solution.py:24
  75.6 0.7 gather_fusion.1
  76.4 1.4 fusion.42
  79.2 12.2 %pmax.7 = f32[16,80]{1,0:T(8,128)S(1)} all-reduce(f32[16,80]{1,0:T(8,128)S(1)} %max.18), channel_id=1, replica_groups=mesh['blk'=8,'req'=4] {'blk'}, use_global_device_ids=true, to_apply=%region_5.6 | all-reduce | flops 1280 | bytes 10240 | tf_op jit(solution)/shard_map/pmax | solution.py:123
  91.5 0.6 gather_fusion.4
  92.0 2.0 %convert_reduce_fusion = f32[16,4,4,5]{3,2,1,0:T(4,128)S(1)} fusion(f32[16,4,4,5,32]{4,3,2,1,0:T(8,128)} %get-tuple-element.11, f32[16,4,4,5]{3,2,1,0:T(4,128)} %copy-done.4, pred[16]{0:T(512)(128)(4,1)} %copy-done.23), kind=kLoop, calls=%fused_computation.22 | loop fusion | flops 203520 | bytes 174096 | tf_op jit(solution)/shard_map/reduce_sum | solution.py:39
  94.1 0.6 copy-done.24
  94.7 2.6 %fusion.10 = f32[16,4,4,5,64]{4,3,2,1,0:T(8,128)} fusion(bf16[16,32,4,64,1]{3,2,1,0,4:T(4,128)(2,1)} %bitcast.87, f32[16,4,4,5,32]{4,3,2,1,0:T(8,128)S(1)} %copy-done.1, f32[16,4,4,5]{3,2,1,0:T(4,128)S(1)} %copy-done.5, pred[16]{0:T(512)(128)(4,1)S(1)} %copy-done.24), kind=kOutput, calls=%fused_computation.26 | convolution fusion | flops 5365760 | bytes 758800 | tf_op jit(solution)/shard_map/rkgnj,rjkd->rkgnd/dot_general | solution.py:114
  97.3 1.5 reshape.319
  100.3 12.6 %all-reduce.2 = f32[16,80]{1,0:T(8,128)} all-reduce(f32[16,80]{1,0:T(8,128)S(1)} %convolution_add_fusion.1), channel_id=4, replica_groups=mesh['blk'=8,'req'=4] {'blk'}, use_global_device_ids=true, to_apply=%region_10.11.clone | all-reduce | flops 1280 | bytes 10240
  113.1 0.8 mul.107
  114.3 0.5 fusion.17
  115.0 0.8 copy-done.3
  115.8 1.1 convolution_add_fusion
  116.9 0.6 copy-done.18
  117.6 0.7 fusion.31
  118.6 49.9 %all-reduce.5.cloned.1.call-done = f32[16,5120]{1,0:T(8,128)} async-done(((f32[16,5120]{1,0:T(8,128)}), f32[16,5120]{1,0:T(8,128)}) %all-reduce.5.cloned.1.call-update) | async-done | bytes 327696
  168.5 0.9 constant_dynamic-slice_fusion
  169.6 0.5 copy-done.13
  170.4 0.7 convert_element_type.56
  (114 shorter events, 8.4 us)
Async XLA Ops:
  6.5 20.5 %copy-start = (s32[1,16]{1,0:T(1,128)S(1)}, s32[1,16]{1,0:T(1,128)}, u32[]{:S(2)}) copy-start(s32[1,16]{1,0:T(1,128)} %param.21) | copy-start | bytes 196
  6.5 162.0 %all-reduce.5.cloned.1.call-start = ((), (), s32[]{:S(2)}) async-start(), calls=%async_computation | async-start | bytes 655360
  6.5 37.8 %collective-permute-start = (bf16[1,1,2,5,1024]{4,2,3,1,0:T(2,128)(2,1)}, bf16[1,1,2,5,1024]{4,2,3,1,0:T(2,128)(2,1)S(1)}, u32[]{:S(2)}, u32[]{:S(2)}) collective-permute-start(bf16[1,1,2,5,1024]{4,2,3,1,0:T(2,128)(2,1)} %bitcast.90), channel_id=1, source_target_pairs={{0,4},{4,0},{8,12},{12,8},{16,20},{20,16},{24,28},{28,24},{1,5},{5... | collective-permute-start | bytes 61448 | tf_op jit(solution)/shard_map/ppermute | solution.py:24
  7.0 0.7 copy-start.20
  7.0 4.3 %copy-start.9 = (bf16[1,2,5,1024]{3,1,2,0:T(2,128)(2,1)S(1)}, bf16[1,2,5,1024]{3,1,2,0:T(2,128)(2,1)}, u32[]{:S(2)}) copy-start(bf16[1,2,5,1024]{3,1,2,0:T(2,128)(2,1)} %param.14) | copy-start | bytes 61444
  7.7 16.6 %copy-start.21 = (s32[8]{0:T(128)}, s32[8]{0:T(128)S(1)}, u32[]{:S(2)}) copy-start(s32[8]{0:T(128)S(1)} %fusion.35) | copy-start | bytes 100
  7.8 0.7 copy-start.25
  8.5 0.7 copy-start.26
  9.1 0.7 copy-start.29
  25.1 0.7 copy-start.14
  25.1 51.2 %copy-start.23 = (pred[16]{0:T(512)(128)(4,1)}, pred[16]{0:T(512)(128)(4,1)S(1)}, u32[]{:S(2)}) copy-start(pred[16]{0:T(512)(128)(4,1)S(1)} %broadcast_compare_fusion) | copy-start | bytes 52
  25.9 0.7 copy-start.15
  28.0 0.7 copy-start.27
  28.7 0.6 copy-start.12
  29.0 0.7 copy-start.7
  29.7 0.8 copy-start.10
  44.4 1.6 copy-start.11
  44.4 25.8 %collective-permute-start.1 = (bf16[2,1,2,5,1024]{4,2,3,0,1:T(2,128)(2,1)S(1)}, bf16[2,1,2,5,1024]{4,2,3,0,1:T(2,128)(2,1)S(1)}, u32[]{:S(2)}, u32[]{:S(2)}) collective-permute-start(bf16[2,1,2,5,1024]{4,2,3,0,1:T(2,128)(2,1)S(1)} %get-tuple-element.9), channel_id=1, source_target_pairs={{0,8},{4,12},{8,0},{12,4},{16,24},{20,28},{24,16},{28,20},{1,9},{5... | collective-permute-start | bytes 122888 | tf_op jit(solution)/shard_map/ppermute | solution.py:24
  61.0 0.7 copy-start.16
  61.8 0.7 copy-start.17
  63.8 2.7 %copy-start.2 = (bf16[1,8,256,256]{3,2,1,0:T(8,128)(2,1)S(1)}, bf16[1,8,256,256]{3,2,1,0:T(8,128)(2,1)}, u32[]{:S(2)}) copy-start(bf16[1,8,256,256]{3,2,1,0:T(8,128)(2,1)} %param.23) | copy-start | bytes 3145732
  68.5 0.7 copy-start.28
  70.5 4.5 %collective-permute-start.2 = (bf16[4,1,2,5,1024]{4,2,0,3,1:T(2,128)(2,1)S(1)}, bf16[4,1,2,5,1024]{4,2,0,3,1:T(2,128)(2,1)S(1)}, u32[]{:S(2)}, u32[]{:S(2)}) collective-permute-start(bf16[4,1,2,5,1024]{4,2,0,3,1:T(2,128)(2,1)S(1)} %copy.57), channel_id=1, source_target_pairs={{0,16},{4,20},{8,24},{12,28},{16,0},{20,4},{24,8},{28,12},{1,17},{... | collective-permute-start | bytes 245768 | tf_op jit(solution)/shard_map/ppermute | solution.py:24
  75.2 1.1 copy-start.6
  77.8 0.7 copy-start.4
  79.0 15.1 %copy-start.1 = (f32[16,4,4,5,32]{4,3,2,1,0:T(8,128)S(1)}, f32[16,4,4,5,32]{4,3,2,1,0:T(8,128)}, u32[]{:S(2)}) copy-start(f32[16,4,4,5,32]{4,3,2,1,0:T(8,128)} %get-tuple-element.11) | copy-start | bytes 491524
  92.0 2.1 %copy-start.5 = (f32[16,4,4,5]{3,2,1,0:T(4,128)S(1)}, f32[16,4,4,5]{3,2,1,0:T(4,128)}, u32[]{:S(2)}) copy-start(f32[16,4,4,5]{3,2,1,0:T(4,128)} %copy-done.4) | copy-start | bytes 15364
  94.1 0.7 copy-start.24
  99.5 0.6 copy-start.22
  114.9 0.9 copy-start.3
  116.9 0.7 copy-start.18
  116.9 0.7 copy-start.19
  118.6 51.0 %copy-start.8 = (f32[2,4,4,5,10]{4,3,2,1,0:T(8,128)S(1)}, f32[2,4,4,5,10]{4,3,2,1,0:T(8,128)}, u32[]{:S(2)}) copy-start(f32[2,4,4,5,10]{4,3,2,1,0:T(8,128)} %copy-done.7) | copy-start | bytes 19204
  169.4 0.7 copy-start.13
Sparse Core Ops, SparseCore 0:
  117.1 51.3 all-reduce.4
